TPU v7x, 32 devices: a whole 2x2x4 slice. The times are simulated.
32 devices in a mesh: dp: 4 (over y, core), blk: 8 (over z, x).
Axes of the slice: x: 2, y: 2, z: 4, core: 2. Of those that a mesh axis runs over, the one named last changes fastest.
Arguments:
- tokens: bfloat16 [4096, 768], P(('dp', 'blk')), may hold values from -6 to 6
- w_qkv: bfloat16 [768, 2304], P(('dp', 'blk')), may hold values from -0.108974863 to 0.108974863
- qv_bias: bfloat16 [2, 768], P(None, ('dp', 'blk')), may hold values from -3 to 3
- w_out: bfloat16 [768, 768], P(('dp', 'blk')), may hold values from -6 to 6
- out_bias: bfloat16 [768], P(('dp', 'blk')), may hold values from -3 to 3
- norm_gain: bfloat16 [2, 768], P(None, ('dp', 'blk')), may hold values from 0.5 to 1.5
- norm_bias: bfloat16 [2, 768], P(None, ('dp', 'blk')), may hold values from -3 to 3
- w_up: bfloat16 [768, 3072], P(('dp', 'blk')), may hold values from -0.21875 to 0.21875
- up_bias: bfloat16 [3072], P(('dp', 'blk')), may hold values from -3 to 3
- w_down: bfloat16 [3072, 768], P(('dp', 'blk')), may hold values from -0.109375 to 0.109375
- down_bias: bfloat16 [768], P(('dp', 'blk')), may hold values from -3 to 3
- cotangent: bfloat16 [4096, 768], P(('dp', 'blk')), may hold values from -6 to 6
Outputs:
- output: bfloat16 [4096, 768], P(('dp', 'blk'))
- d_tokens: float32 [4096, 768], P(('dp', 'blk'))
- d_w_qkv: float32 [768, 2304], P(('dp', 'blk'))
- d_qv_bias: float32 [2, 768], P(None, ('dp', 'blk'))
- d_w_out: float32 [768, 768], P(('dp', 'blk'))
- d_out_bias: float32 [768], P(('dp', 'blk'))
- d_norm_gain: float32 [2, 768], P(None, ('dp', 'blk'))
- d_norm_bias: float32 [2, 768], P(None, ('dp', 'blk'))
- d_w_up: float32 [768, 3072], P(('dp', 'blk'))
- d_up_bias: float32 [3072], P(('dp', 'blk'))
- d_w_down: float32 [3072, 768], P(('dp', 'blk'))
- d_down_bias: float32 [768], P(('dp', 'blk'))
All inputs are finite; a program needn't handle non-finite values.
Results may differ from a plain program's by a relative error of at most 0.014.
Values may be sent and summed in bfloat16 or wider, within the bound.
A program may use at most 192 MiB of HBM per device.

v0:
```python
import jax
import jax.numpy as jnp
from jax import lax
from jax.sharding import PartitionSpec as P

HEAD = 64


EPS = 1e-05
SCALE = 0.125


def layernorm_forward(h, norm_gain_vector, norm_offset):
    row_average = jnp.mean(h, axis=-1, keepdims=True)
    centered_input = h - row_average
    var = jnp.mean(centered_input * centered_input, axis=-1, keepdims=True)
    inverse_deviation = lax.rsqrt(var + EPS)
    normalized_input = centered_input * inverse_deviation
    return (normalized_input * norm_gain_vector + norm_offset, normalized_input, inverse_deviation)


def layernorm_backward(incoming_gradient, normalized_input, inverse_deviation, norm_gain_vector):
    scaled_values = incoming_gradient * norm_gain_vector
    return inverse_deviation * (
        scaled_values
        - jnp.mean(scaled_values, axis=-1, keepdims=True)
        - normalized_input * jnp.mean(scaled_values * normalized_input, axis=-1, keepdims=True)
    )


def gelu_grad(up):
    cdf = 0.5 * (1.0 + jax.scipy.special.erf(up * 0.7071067811865476))
    return cdf + up * jnp.exp(-0.5 * up * up) * 0.3989422804014327


def contract_rows(left, right):
    return lax.dot_general(
        left, right, (((0,), (0,)), ((), ())), preferred_element_type=jnp.float32
    )


def contract_cols(left, right):
    return lax.dot_general(
        left, right, (((1,), (1,)), ((), ())), preferred_element_type=jnp.float32
    )


def on_device(
    tokens,
    w_qkv,
    qv_bias,
    w_out,
    out_bias,
    norm_gain,
    norm_bias,
    w_up,
    up_bias,
    w_down,
    down_bias,
    cotangent,
):
    f32 = jnp.float32
    bf16 = jnp.bfloat16
    rows, width = tokens.shape
    heads = width // HEAD
    full = (
        lax.all_gather(w_qkv, ("dp", "blk"), axis=0, tiled=True),
        lax.all_gather(qv_bias, ("dp", "blk"), axis=1, tiled=True),
        lax.all_gather(w_out, ("dp", "blk"), axis=0, tiled=True),
        lax.all_gather(out_bias, ("dp", "blk"), axis=0, tiled=True),
        lax.all_gather(norm_gain, ("dp", "blk"), axis=1, tiled=True),
        lax.all_gather(norm_bias, ("dp", "blk"), axis=1, tiled=True),
        lax.all_gather(w_up, ("dp", "blk"), axis=0, tiled=True),
        lax.all_gather(up_bias, ("dp", "blk"), axis=0, tiled=True),
        lax.all_gather(w_down, ("dp", "blk"), axis=0, tiled=True),
        lax.all_gather(down_bias, ("dp", "blk"), axis=0, tiled=True),
    )
    (
        wq_full,
        qvb_full,
        wo_full,
        bo_full,
        gain_full,
        shift_full,
        wu_full,
        bu_full,
        wd_full,
        bd_full,
    ) = full
    norm_gain_pair = gain_full.astype(f32)
    norm_offset_pair = shift_full.astype(f32)
    qvb = qvb_full.astype(f32)
    bias_row = jnp.concatenate([qvb[0], jnp.zeros((width,), f32), qvb[1]])
    qkv = (jnp.dot(tokens, wq_full, preferred_element_type=f32) + bias_row).astype(bf16)
    query = qkv[:, :width]
    keys_own = qkv[:, width : 2 * width]
    values_own = qkv[:, 2 * width :]
    init = (
        jnp.full((heads, rows), -1e30, f32),
        jnp.zeros((heads, rows), f32),
        jnp.zeros((rows, width), f32),
    )
    keys = lax.all_gather(keys_own, "blk", axis=0, tiled=True)
    values = lax.all_gather(values_own, "blk", axis=0, tiled=True)

    def per_head(h, state):
        peak, total, accum = state
        q_h = lax.dynamic_slice_in_dim(query, h * HEAD, HEAD, 1)
        k_h = lax.dynamic_slice_in_dim(keys, h * HEAD, HEAD, 1)
        v_h = lax.dynamic_slice_in_dim(values, h * HEAD, HEAD, 1)
        scores = contract_cols(q_h, k_h) * SCALE
        old = peak[h]
        new = jnp.maximum(old, jnp.max(scores, axis=1))
        fade = jnp.exp(old - new)
        weights = jnp.exp(scores - new[:, None])
        total = total.at[h].set(total[h] * fade + jnp.sum(weights, axis=1))
        part = jnp.dot(weights.astype(bf16), v_h, preferred_element_type=f32)
        acc_h = lax.dynamic_slice_in_dim(accum, h * HEAD, HEAD, 1) * fade[:, None] + part
        accum = lax.dynamic_update_slice_in_dim(accum, acc_h, h * HEAD, 1)
        peak = peak.at[h].set(new)
        return (peak, total, accum)

    peak, total, accum = lax.fori_loop(0, heads, per_head, init)
    lse = peak + jnp.log(total)
    attn = (accum / jnp.repeat(total.T, HEAD, axis=1)).astype(bf16)
    first_hidden = (
        tokens.astype(f32)
        + jnp.dot(attn, wo_full, preferred_element_type=f32)
        + bo_full.astype(f32)
    )
    first_norm_output, first_normalized, first_inverse_deviation = layernorm_forward(
        first_hidden, norm_gain_pair[0], norm_offset_pair[0]
    )
    y1_low = first_norm_output.astype(bf16)
    up = jnp.dot(y1_low, wu_full, preferred_element_type=f32) + bu_full.astype(f32)
    act = jax.nn.gelu(up, approximate=False).astype(bf16)
    second_hidden = (
        first_norm_output + jnp.dot(act, wd_full, preferred_element_type=f32) + bd_full.astype(f32)
    )
    output_float, second_normalized, second_inverse_deviation = layernorm_forward(
        second_hidden, norm_gain_pair[1], norm_offset_pair[1]
    )
    output = output_float.astype(bf16)
    again = (
        lax.all_gather(w_qkv, ("dp", "blk"), axis=0, tiled=True),
        lax.all_gather(qv_bias, ("dp", "blk"), axis=1, tiled=True),
        lax.all_gather(w_out, ("dp", "blk"), axis=0, tiled=True),
        lax.all_gather(out_bias, ("dp", "blk"), axis=0, tiled=True),
        lax.all_gather(norm_gain, ("dp", "blk"), axis=1, tiled=True),
        lax.all_gather(norm_bias, ("dp", "blk"), axis=1, tiled=True),
        lax.all_gather(w_up, ("dp", "blk"), axis=0, tiled=True),
        lax.all_gather(up_bias, ("dp", "blk"), axis=0, tiled=True),
        lax.all_gather(w_down, ("dp", "blk"), axis=0, tiled=True),
        lax.all_gather(down_bias, ("dp", "blk"), axis=0, tiled=True),
    )
    wq_b, wo_b, wu_b, wd_b = (again[0], again[2], again[6], again[8])
    gain_pair_block = again[4].astype(f32)
    incoming_gradient = cotangent.astype(f32)
    second_gain_gradient = jnp.sum(incoming_gradient * second_normalized, axis=0)
    d_shift2 = jnp.sum(incoming_gradient, axis=0)
    second_hidden_gradient = layernorm_backward(
        incoming_gradient, second_normalized, second_inverse_deviation, gain_pair_block[1]
    )
    dh2_low = second_hidden_gradient.astype(bf16)
    d_w_down = contract_rows(act, dh2_low)
    d_down_bias = jnp.sum(second_hidden_gradient, axis=0)
    d_up_f = contract_cols(dh2_low, wd_b) * gelu_grad(up)
    d_up_bias = jnp.sum(d_up_f, axis=0)
    d_up = d_up_f.astype(bf16)
    d_w_up = contract_rows(y1_low, d_up)
    first_output_gradient = second_hidden_gradient + contract_cols(d_up, wu_b)
    first_gain_gradient = jnp.sum(first_output_gradient * first_normalized, axis=0)
    d_shift1 = jnp.sum(first_output_gradient, axis=0)
    first_hidden_gradient = layernorm_backward(
        first_output_gradient, first_normalized, first_inverse_deviation, gain_pair_block[0]
    )
    dh1_low = first_hidden_gradient.astype(bf16)
    d_w_out = contract_rows(attn, dh1_low)
    d_out_bias = jnp.sum(first_hidden_gradient, axis=0)
    d_gains = jnp.stack([first_gain_gradient, second_gain_gradient])
    d_shifts = jnp.stack([d_shift1, d_shift2])
    d_attn = contract_cols(dh1_low, wo_b).astype(bf16)
    delta = jnp.sum((d_attn.astype(f32) * attn.astype(f32)).reshape(rows, heads, HEAD), axis=-1).T
    span = rows * lax.axis_size("blk")
    init_back = (jnp.zeros((rows, width), f32), jnp.zeros((span, 2 * width), f32))
    start = jnp.int32(0)
    attend_keys = lax.all_gather(keys_own, "blk", axis=0, tiled=True)
    attend_values = lax.all_gather(values_own, "blk", axis=0, tiled=True)
    count = attend_keys.shape[0]

    def per_head(h, state):
        d_query, d_kv = state
        q_h = lax.dynamic_slice_in_dim(query, h * HEAD, HEAD, 1)
        k_h = lax.dynamic_slice_in_dim(attend_keys, h * HEAD, HEAD, 1)
        v_h = lax.dynamic_slice_in_dim(attend_values, h * HEAD, HEAD, 1)
        do_h = lax.dynamic_slice_in_dim(d_attn, h * HEAD, HEAD, 1)
        scores = contract_cols(q_h, k_h) * SCALE
        probs = jnp.exp(scores - lse[h][:, None])
        dprobs = contract_cols(do_h, v_h)
        dscores = (probs * (dprobs - delta[h][:, None])).astype(bf16)
        dq_h = lax.dynamic_slice_in_dim(d_query, h * HEAD, HEAD, 1) + SCALE * jnp.dot(
            dscores, k_h, preferred_element_type=f32
        )
        d_query = lax.dynamic_update_slice_in_dim(d_query, dq_h, h * HEAD, 1)
        dk_h = SCALE * contract_rows(dscores, q_h)
        dv_h = contract_rows(probs.astype(bf16), do_h)
        key_col = h * HEAD
        val_col = width + h * HEAD
        old_k = lax.dynamic_slice(d_kv, (start, key_col), (count, HEAD))
        d_kv = lax.dynamic_update_slice(d_kv, old_k + dk_h, (start, key_col))
        old_v = lax.dynamic_slice(d_kv, (start, val_col), (count, HEAD))
        d_kv = lax.dynamic_update_slice(d_kv, old_v + dv_h, (start, val_col))
        return (d_query, d_kv)

    d_query, d_kv_all = lax.fori_loop(0, heads, per_head, init_back)
    d_kv = lax.psum_scatter(
        d_kv_all.astype(jnp.bfloat16), "blk", scatter_dimension=0, tiled=True
    ).astype(jnp.float32)
    d_key = d_kv[:, :width]
    d_value = d_kv[:, width:]
    d_qv = jnp.stack([jnp.sum(d_query, axis=0), jnp.sum(d_value, axis=0)])
    d_qkv = jnp.concatenate([d_query, d_key, d_value], axis=1).astype(bf16)
    d_w_qkv = contract_rows(tokens, d_qkv)
    d_tokens = first_hidden_gradient + contract_cols(d_qkv, wq_b)
    parts = (
        lax.psum_scatter(d_w_qkv, ("dp", "blk"), scatter_dimension=0, tiled=True),
        lax.psum_scatter(d_qv, ("dp", "blk"), scatter_dimension=1, tiled=True),
        lax.psum_scatter(d_w_out, ("dp", "blk"), scatter_dimension=0, tiled=True),
        lax.psum_scatter(d_out_bias, ("dp", "blk"), scatter_dimension=0, tiled=True),
        lax.psum_scatter(d_gains, ("dp", "blk"), scatter_dimension=1, tiled=True),
        lax.psum_scatter(d_shifts, ("dp", "blk"), scatter_dimension=1, tiled=True),
        lax.psum_scatter(d_w_up, ("dp", "blk"), scatter_dimension=0, tiled=True),
        lax.psum_scatter(d_up_bias, ("dp", "blk"), scatter_dimension=0, tiled=True),
        lax.psum_scatter(d_w_down, ("dp", "blk"), scatter_dimension=0, tiled=True),
        lax.psum_scatter(d_down_bias, ("dp", "blk"), scatter_dimension=0, tiled=True),
    )
    g_wqkv, g_qv, g_wout, g_bout, g_gain, g_shift, g_wup, g_bup, g_wdown, g_bdown = parts
    return (
        output,
        d_tokens,
        g_wqkv,
        g_qv,
        g_wout,
        g_bout,
        g_gain,
        g_shift,
        g_wup,
        g_bup,
        g_wdown,
        g_bdown,
    )


def solution(mesh):
    return jax.shard_map(
        on_device,
        mesh=mesh,
        in_specs=(
            P(("dp", "blk"), None),
            P(("dp", "blk"), None),
            P(None, ("dp", "blk")),
            P(("dp", "blk"), None),
            P(("dp", "blk")),
            P(None, ("dp", "blk")),
            P(None, ("dp", "blk")),
            P(("dp", "blk"), None),
            P(("dp", "blk")),
            P(("dp", "blk"), None),
            P(("dp", "blk")),
            P(("dp", "blk"), None),
        ),
        out_specs=(
            P(("dp", "blk"), None),
            P(("dp", "blk"), None),
            P(("dp", "blk"), None),
            P(None, ("dp", "blk")),
            P(("dp", "blk"), None),
            P(("dp", "blk")),
            P(None, ("dp", "blk")),
            P(None, ("dp", "blk")),
            P(("dp", "blk"), None),
            P(("dp", "blk")),
            P(("dp", "blk"), None),
            P(("dp", "blk")),
        ),
        check_vma=False,
    )
```

profile of v0, /device:TPU:0, one launch (start us, length us, event | category | flops | bytes accessed | tf_op | source)
XLA Modules:
  0.0 1063.2 jit_solution(13943447860457645288)
XLA Ops:
  8.0 70.1 %all-gather = bf16[32,24,2]{1,2,0:T(2,128)(2,1)S(1)} all-gather(bf16[1,24,2]{1,2,0:T(2,128)(2,1)} %bitcast.98), channel_id=1, replica_groups=mesh['dp'=4,'blk'=8] {'dp','blk'}, dimensions={0}, use_global_device_ids=true | all-gather | bytes 3168 | tf_op jit(solution)/shard_map/all_gather | solution.py:68
  78.4 2.8 fusion.37
  85.4 37.9 %all-reduce.10 = (bf16[3072]{0:T(1024)(128)(2,1)S(1)}, bf16[768]{0:T(1024)(128)(2,1)S(1)}, bf16[768]{0:T(1024)(128)(2,1)S(1)}) all-reduce(bf16[3072]{0:T(1024)(128)(2,1)S(1)} %dynamic-update-slice.15, bf16[768]{0:T(1024)(128)(2,1)S(1)} %dynamic-update-slice.14, ...), channel_id=1, replica_groups=mesh['dp'=4,'blk'=8] {'dp','blk'}, use_global_device_ids=true, to_apply=%add.1 | all-reduce | flops 4608 | bytes 18432
  123.3 65.9 %all-gather.1 = bf16[32,24,2]{1,2,0:T(2,128)(2,1)S(1)} all-gather(bf16[1,24,2]{1,2,0:T(2,128)(2,1)S(1)} %bitcast.99), channel_id=1, replica_groups=mesh['dp'=4,'blk'=8] {'dp','blk'}, dimensions={0}, use_global_device_ids=true | all-gather | bytes 3168 | tf_op jit(solution)/shard_map/all_gather | solution.py:71
  189.3 63.5 %all-gather.2 = bf16[32,24,2]{1,2,0:T(2,128)(2,1)S(1)} all-gather(bf16[1,24,2]{1,2,0:T(2,128)(2,1)S(1)} %bitcast.100), channel_id=1, replica_groups=mesh['dp'=4,'blk'=8] {'dp','blk'}, dimensions={0}, use_global_device_ids=true | all-gather | bytes 3168 | tf_op jit(solution)/shard_map/all_gather | solution.py:72
  253.5 53.2 %while.36 = (s32[]{:T(128)}, f32[12,128]{1,0:T(8,128)S(1)}, f32[12,128]{1,0:T(8,128)S(1)}, f32[128,768]{0,1:T(8,128)S(1)}, bf16[128,768]{1,0:T(8,128)(2,1)S(1)},...) while((s32[]{:T(128)}, f32[12,128]{1,0:T(8,128)S(1)}, ...), condition=%wide.region_4.5_spmd, body=%wide.region_0.4_spmd.sunk | while | flops 34358160 | bytes 2208981 | solution.py:123
  309.6 7.7 fusion.40
  317.3 36.7 %all-gather.20.cloned.1.call-done = bf16[3072,768]{1,0:T(8,128)(2,1)} async-done(((bf16[96,768]{1,0:T(8,128)(2,1)}), bf16[3072,768]{1,0:T(8,128)(2,1)}) %all-gather.20.cloned.1.call-update) | async-done | bytes 4718608 | tf_op jit(solution)/shard_map/all_gather | solution.py:75
  354.0 3.4 fusion.82
  359.9 2.3 fusion.83
  362.2 2.3 multiply_reduce_fusion
  366.9 3.5 broadcast_in_dim.24
  370.4 93.8 %while.37 = (s32[]{:T(128)}, f32[128,768]{0,1:T(8,128)S(1)}, f32[1024,1536]{0,1:T(8,128)}, bf16[128,768]{1,0:T(8,128)(2,1)S(1)}, bf16[1024,768]{1,0:T(8,128)(2,1...) while((s32[]{:T(128)}, f32[128,768]{0,1:T(8,128)S(1)}, ...), condition=%wide.region_15.0_spmd, body=%wide.region_14.0_spmd.sunk | while | flops 84885504 | bytes 4397330 | solution.py:215
  397.7 2.0 fusion.144
  405.5 2.0 fusion.144
  413.3 2.0 fusion.144
  430.9 2.0 fusion.145
  436.7 2.0 fusion.144
  460.2 2.0 fusion.144
  464.9 3.3 convert_element_type.109
  468.2 3.0 copy.51
  475.2 5.1 fusion.61
  481.6 5.1 fusion.68
  487.9 56.0 %reduce-scatter.19.cloned.1.call-done = bf16[128,1536]{1,0:T(8,128)(2,1)} async-done(((bf16[1024,1536]{1,0:T(8,128)(2,1)}), bf16[128,1536]{1,0:T(8,128)(2,1)}) %reduce-scatter.19.cloned.1.call-update) | async-done | bytes 393232
  545.2 4.0 convolution_bitcast_fusion
  549.1 8.0 copy.53
  560.6 41.5 %all-reduce.9 = (f32[2,768]{1,0:T(2,128)}, f32[768]{0:T(1024)}, f32[2,768]{1,0:T(2,128)}, f32[2,768]{1,0:T(2,128)}, f32[3072]{0:T(1024)}, /*index=5*/f32[768]{0:T(1024)}) all-reduce(f32[2,768]{1,0:T(2,128)} %pad_maximum_fusion.4, f32[768]{0:T(1024)} %get-tuple-element.515, ...), channel_id=4, replica_groups=mesh['dp'=4,'blk'=8] {'dp','blk'}, use_global_device_ids=true, to_apply=%region_20.0.clone | all-reduce | flops 9216 | bytes 73728
  609.8 3.2 convolution_add_fusion.5
  613.0 35.7 %reduce-scatter.13.cloned.1.call-done = f32[24,768]{1,0:T(8,128)} async-done(((f32[768,768]{1,0:T(8,128)}), f32[24,768]{1,0:T(8,128)}) %reduce-scatter.13.cloned.1.call-update) | async-done | bytes 73744 | tf_op jit(solution)/shard_map/reduce_scatter | solution.py:228
  648.7 141.7 %reduce-scatter.15.cloned.1.call-done = f32[24,3072]{1,0:T(8,128)} async-done(((f32[768,3072]{1,0:T(8,128)}), f32[24,3072]{1,0:T(8,128)}) %reduce-scatter.15.cloned.1.call-update) | async-done | bytes 294928 | tf_op jit(solution)/shard_map/reduce_scatter | solution.py:232
  790.3 141.5 %reduce-scatter.17.cloned.1.call-done = f32[96,768]{1,0:T(8,128)} async-done(((f32[3072,768]{1,0:T(8,128)}), f32[96,768]{1,0:T(8,128)}) %reduce-scatter.17.cloned.1.call-update) | async-done | bytes 294928 | tf_op jit(solution)/shard_map/reduce_scatter | solution.py:234
  931.9 124.8 %reduce-scatter.21.cloned.1.call-done = f32[24,2304]{1,0:T(8,128)} async-done(((f32[768,2304]{1,0:T(8,128)}), f32[24,2304]{1,0:T(8,128)}) %reduce-scatter.21.cloned.1.call-update) | async-done | bytes 221200
  (339 shorter events, 166.9 us)
Async XLA Ops:
  7.2 71.3 %all-gather.10.cloned.1.call-start = ((), (), s32[]{:S(2)}) async-start(), calls=%async_computation.5 | async-start | bytes 3649536 | tf_op jit(solution)/shard_map/all_gather | solution.py:67
  7.9 245.5 %all-gather.14.cloned.1.call-start = ((), (), s32[]{:S(2)}) async-start(), calls=%async_computation.7 | async-start | bytes 1769472 | tf_op jit(solution)/shard_map/all_gather | solution.py:104
  81.2 3.4 copy-start.26
  81.2 3.7 copy-start.27
  81.2 3.9 copy-start.28
  81.2 42.1 %copy-start.24 = (bf16[2,24]{1,0:T(2,128)(2,1)S(1)}, bf16[2,24]{1,0:T(2,128)(2,1)}, u32[]{:S(2)}) copy-start(bf16[2,24]{1,0:T(2,128)(2,1)} %param.25) | copy-start | bytes 292
  81.3 108.1 %copy-start.25 = (bf16[2,24]{1,0:T(2,128)(2,1)S(1)}, bf16[2,24]{1,0:T(2,128)(2,1)}, u32[]{:S(2)}) copy-start(bf16[2,24]{1,0:T(2,128)(2,1)} %param.26) | copy-start | bytes 292
  81.3 172.2 %copy-start.21 = (s32[2]{0:T(128)S(1)}, s32[2]{0:T(128)}, u32[]{:S(2)}) copy-start(s32[2]{0:T(128)} %constant.238.clone.1) | copy-start | bytes 28
  82.1 171.3 %all-gather.12.cloned.1.call-start = ((), (), s32[]{:S(2)}) async-start(), calls=%async_computation.6 | async-start | bytes 1769472 | tf_op jit(solution)/shard_map/all_gather | solution.py:103
  82.8 224.4 %all-gather.16.cloned.1.call-start = ((), (), s32[]{:S(2)}) async-start(), calls=%async_computation.8 | async-start | bytes 1216512 | tf_op jit(solution)/shard_map/all_gather | solution.py:69
  83.4 226.2 %all-gather.18.cloned.1.call-start = ((), (), s32[]{:S(2)}) async-start(), calls=%async_computation.9 | async-start | bytes 4866048 | tf_op jit(solution)/shard_map/all_gather | solution.py:73
  84.0 270.0 %all-gather.20.cloned.1.call-start = ((), (), s32[]{:S(2)}) async-start(), calls=%async_computation.10 | async-start | bytes 4866048 | tf_op jit(solution)/shard_map/all_gather | solution.py:75
  84.6 459.4 %reduce-scatter.19.cloned.1.call-start = ((), (), s32[]{:S(2)}) async-start(), calls=%async_computation.14 | async-start | bytes 3538944
  307.2 58.2 %copy-start.9 = (bf16[128,768]{1,0:T(8,128)(2,1)}, bf16[128,768]{1,0:T(8,128)(2,1)S(1)}, u32[]{:S(2)}) copy-start(bf16[128,768]{1,0:T(8,128)(2,1)S(1)} %divide_convert_fusion) | copy-start | bytes 589828
  309.6 55.0 %copy-start.22 = (f32[128]{0:T(128)}, f32[128]{0:T(128)S(1)}, u32[]{:S(2)}) copy-start(f32[128]{0:T(128)S(1)} %add_rsqrt_fusion.1) | copy-start | bytes 1540
  317.3 40.1 %copy-start.5 = (bf16[128,3072]{1,0:T(8,128)(2,1)}, bf16[128,3072]{1,0:T(8,128)(2,1)S(1)}, u32[]{:S(2)}) copy-start(bf16[128,3072]{1,0:T(8,128)(2,1)S(1)} %get-tuple-element.531) | copy-start | bytes 2359300
  354.0 5.9 slice-start
  354.0 3.6 copy-start.18
  354.0 5.9 slice-start.1
  357.4 2.5 copy-start.29
  358.4 3.8 slice-start.2
  359.9 2.4 copy-start.7
  359.9 2.3 slice-start.3
  362.2 2.4 copy-start.11
  471.2 177.5 %reduce-scatter.13.cloned.1.call-start = ((), (), s32[]{:S(2)}) async-start(), calls=%async_computation.11 | async-start | bytes 2433024 | tf_op jit(solution)/shard_map/reduce_scatter | solution.py:228
  474.1 316.2 %reduce-scatter.15.cloned.1.call-start = ((), (), s32[]{:S(2)}) async-start(), calls=%async_computation.12 | async-start | bytes 9732096 | tf_op jit(solution)/shard_map/reduce_scatter | solution.py:232
  480.4 451.5 %reduce-scatter.17.cloned.1.call-start = ((), (), s32[]{:S(2)}) async-start(), calls=%async_computation.13 | async-start | bytes 9732096 | tf_op jit(solution)/shard_map/reduce_scatter | solution.py:234
  486.7 58.5 %copy-start.16 = (bf16[128,768]{1,0:T(8,128)(2,1)S(1)}, bf16[128,768]{1,0:T(8,128)(2,1)}, u32[]{:S(2)}) copy-start(bf16[128,768]{1,0:T(8,128)(2,1)} %param.20) | copy-start | bytes 589828
  486.7 569.9 %reduce-scatter.21.cloned.1.call-start = ((), (), s32[]{:S(2)}) async-start(), calls=%async_computation.15 | async-start | bytes 7299072
  487.9 61.2 %copy-start.17 = (bf16[128,768]{0,1:T(8,128)(2,1)}, bf16[128,768]{0,1:T(8,128)(2,1)S(1)}, u32[]{:S(2)}) copy-start(bf16[128,768]{0,1:T(8,128)(2,1)S(1)} %get-tuple-element.528) | copy-start | bytes 589828
  545.1 4.0 copy-start.3
  557.2 52.6 %copy-start = (bf16[768,2304]{1,0:T(8,128)(2,1)S(1)}, bf16[768,2304]{1,0:T(8,128)(2,1)}, u32[]{:S(2)}) copy-start(bf16[768,2304]{1,0:T(8,128)(2,1)} %all-gather.10.cloned.1.call-done) | copy-start | bytes 10616836
  (13 other events, 14.0 us)
Sparse Core Ops, SparseCore 0:
  11.0 62.8 all-gather.9
  82.2 40.5 all-gather.13
  125.5 42.6 all-gather.11
  171.0 52.4 all-gather.15
  226.3 62.5 all-gather.17
  291.8 62.1 all-gather.19
  471.3 72.5 reduce-scatter.18
  549.8 98.8 reduce-scatter.12
  655.2 135.1 reduce-scatter.14
  796.7 135.1 reduce-scatter.16
  938.1 118.4 reduce-scatter.20
where the time goes:
time: 1070 us; the launch traced here: 1060 us
  waiting for transfers between devices  540 us (50%)
  blocking collectives  279 us (26%)
  matrix products  166 us (16%)
  local copies, waits for them, and re-layouts  35.1 us (3%)
  other arithmetic  28 us (3%)
  between operations  14.4 us (1%)
    unnamed x13, waiting for transfers between devices  184 us
    reduce_scatter x1, waiting for transfers between devices, on_device(): lax.psum_scatter(d_w_up, ('dp', 'blk'), scatter_dimension=0, tiled=True)  142 us
    reduce_scatter x1, waiting for transfers between devices, on_device(): lax.psum_scatter(d_w_down, ('dp', 'blk'), scatter_dimension=0, tiled=True)  142 us
    unnamed x2, blocking collectives  79.4 us
    all_gather x1, blocking collectives, on_device(): lax.all_gather(qv_bias, ('dp', 'blk'), axis=1, tiled=True)  70.1 us
    all_gather x1, blocking collectives, on_device(): lax.all_gather(norm_gain, ('dp', 'blk'), axis=1, tiled=True)  65.9 us
    all_gather x1, blocking collectives, on_device(): lax.all_gather(norm_bias, ('dp', 'blk'), axis=1, tiled=True)  63.5 us
    dot_general x28, matrix products, contract_rows(): lax.dot_general(left, right, (((0,), (0,)), ((), ())), preferred_element_...  63.1 us
  transfers between devices with their start and end apart: 11, of which 6 were waited for; matrix products, arithmetic and copies ran while one was open for 10% of the time, Pallas kernels for 0%

commit v1 on v0

v1 whole, which is shorter than its diff:
```python
import functools

import jax
import jax.numpy as jnp
from jax import lax
from jax.experimental import pallas as pl
from jax.experimental.pallas import tpu as pltpu
from jax.sharding import PartitionSpec as P

HEAD = 64


EPS = 1e-05
SCALE = 0.125


def layernorm_forward(h, norm_gain_vector, norm_offset):
    row_average = jnp.mean(h, axis=-1, keepdims=True)
    centered_input = h - row_average
    var = jnp.mean(centered_input * centered_input, axis=-1, keepdims=True)
    inverse_deviation = lax.rsqrt(var + EPS)
    normalized_input = centered_input * inverse_deviation
    return (normalized_input * norm_gain_vector + norm_offset, normalized_input, inverse_deviation)


def layernorm_backward(incoming_gradient, normalized_input, inverse_deviation, norm_gain_vector):
    scaled_values = incoming_gradient * norm_gain_vector
    return inverse_deviation * (
        scaled_values
        - jnp.mean(scaled_values, axis=-1, keepdims=True)
        - normalized_input * jnp.mean(scaled_values * normalized_input, axis=-1, keepdims=True)
    )


def gelu_grad(up):
    cdf = 0.5 * (1.0 + jax.scipy.special.erf(up * 0.7071067811865476))
    return cdf + up * jnp.exp(-0.5 * up * up) * 0.3989422804014327


def contract_rows(left, right):
    return lax.dot_general(
        left, right, (((0,), (0,)), ((), ())), preferred_element_type=jnp.float32
    )


def contract_cols(left, right):
    return lax.dot_general(
        left, right, (((1,), (1,)), ((), ())), preferred_element_type=jnp.float32
    )


PAIR = 2 * HEAD


def attend_kernel(width, q_ref, kv_ref, attn_ref, lse_ref):
    def pair(i, carry):
        at = pl.ds(pl.multiple_of(i * PAIR, PAIR), PAIR)
        q2 = q_ref[:, at]
        k2 = kv_ref[:, at]
        v2 = kv_ref[:, pl.ds(pl.multiple_of(width + i * PAIR, PAIR), PAIR)]
        outs, logs = [], []
        for j in range(2):
            own = slice(j * HEAD, (j + 1) * HEAD)
            scores = contract_cols(q2[:, own], k2[:, own]) * SCALE
            peak = jnp.max(scores, axis=1, keepdims=True)
            weights = jnp.exp(scores - peak)
            total = jnp.sum(weights, axis=1, keepdims=True)
            part = jnp.dot(
                weights.astype(jnp.bfloat16), v2[:, own], preferred_element_type=jnp.float32
            )
            outs.append((part / total).astype(jnp.bfloat16))
            logs.append(peak + jnp.log(total))
        attn_ref[:, at] = jnp.concatenate(outs, axis=1)
        lse_ref[i] = jnp.concatenate(logs, axis=1)
        return carry

    lax.fori_loop(0, width // PAIR, pair, 0)


def attend(query, kv):
    rows, width = query.shape
    vmem = pl.BlockSpec(memory_space=pltpu.VMEM)
    return pl.pallas_call(
        functools.partial(attend_kernel, width),
        out_shape=(
            jax.ShapeDtypeStruct((rows, width), jnp.bfloat16),
            jax.ShapeDtypeStruct((width // PAIR, rows, 2), jnp.float32),
        ),
        in_specs=[vmem] * 2,
        out_specs=(vmem, vmem),
        compiler_params=pltpu.CompilerParams(vmem_limit_bytes=60 << 20),
    )(query, kv)


def attend_back_kernel(width, q_ref, kv_ref, do_ref, lse_ref, delta_ref, dq_ref, dkv_ref):
    def pair(i, carry):
        at = pl.ds(pl.multiple_of(i * PAIR, PAIR), PAIR)
        val = pl.ds(pl.multiple_of(width + i * PAIR, PAIR), PAIR)
        q2 = q_ref[:, at]
        do2 = do_ref[:, at]
        k2 = kv_ref[:, at]
        v2 = kv_ref[:, val]
        lse2 = lse_ref[i]
        delta2 = delta_ref[i]
        dqs, dks, dvs = [], [], []
        for j in range(2):
            own = slice(j * HEAD, (j + 1) * HEAD)
            q_h, do_h, k_h, v_h = q2[:, own], do2[:, own], k2[:, own], v2[:, own]
            scores = contract_cols(k_h, q_h) * SCALE
            probs = jnp.exp(scores - lse2[j : j + 1])
            dprobs = contract_cols(v_h, do_h)
            dscores = (probs * (dprobs - delta2[j : j + 1])).astype(jnp.bfloat16)
            dqs.append(SCALE * contract_rows(dscores, k_h))
            dks.append(SCALE * jnp.dot(dscores, q_h, preferred_element_type=jnp.float32))
            dvs.append(
                jnp.dot(probs.astype(jnp.bfloat16), do_h, preferred_element_type=jnp.float32)
            )
        dq_ref[:, at] = jnp.concatenate(dqs, axis=1)
        dkv_ref[:, at] = jnp.concatenate(dks, axis=1).astype(jnp.bfloat16)
        dkv_ref[:, val] = jnp.concatenate(dvs, axis=1).astype(jnp.bfloat16)
        return carry

    lax.fori_loop(0, width // PAIR, pair, 0)


def attend_back(query, kv, d_attn, lse, delta):
    rows, width = query.shape
    vmem = pl.BlockSpec(memory_space=pltpu.VMEM)
    return pl.pallas_call(
        functools.partial(attend_back_kernel, width),
        out_shape=(
            jax.ShapeDtypeStruct((rows, width), jnp.float32),
            jax.ShapeDtypeStruct(kv.shape, jnp.bfloat16),
        ),
        in_specs=[vmem] * 5,
        out_specs=(vmem, vmem),
        compiler_params=pltpu.CompilerParams(vmem_limit_bytes=60 << 20),
    )(query, kv, d_attn, lse, delta)


SPARE = 8


def split_owner(full, count):
    p = full.shape[0]
    return full.reshape(p, count, -1).transpose(1, 0, 2).reshape(count, -1)


def join_owner(parts, p):
    count = parts.shape[0]
    return parts.reshape(count, p, -1).transpose(1, 0, 2).reshape(p, -1)


def on_device(
    tokens,
    w_qkv,
    qv_bias,
    w_out,
    out_bias,
    norm_gain,
    norm_bias,
    w_up,
    up_bias,
    w_down,
    down_bias,
    cotangent,
):
    f32 = jnp.float32
    bf16 = jnp.bfloat16
    rows, width = tokens.shape
    heads = width // HEAD
    n = lax.axis_size("dp") * lax.axis_size("blk")
    own_rows, wide = w_qkv.shape
    small = [qv_bias, out_bias, norm_gain, norm_bias, up_bias, down_bias]
    sizes = [v.size for v in small]
    row = jnp.concatenate([v.reshape(-1) for v in small])
    row = jnp.pad(row[None], ((0, SPARE - 1), (0, wide - row.size)))
    packed = lax.all_gather(jnp.concatenate([w_qkv, row]), ("dp", "blk"), axis=0)
    wq_full = packed[:, :own_rows].reshape(width, wide)
    row_full = packed[:, own_rows]
    parts, at = [], 0
    for size, v in zip(sizes, small):
        parts.append(join_owner(row_full[:, at : at + size], 2 if v.ndim == 2 else 1))
        at += size
    qvb_full, bo_full, gain_full, shift_full, bu_full, bd_full = parts
    bo_full, bu_full, bd_full = bo_full[0], bu_full[0], bd_full[0]
    wo_full = lax.all_gather(w_out, ("dp", "blk"), axis=0, tiled=True)
    wu_full = lax.all_gather(w_up, ("dp", "blk"), axis=0, tiled=True)
    wd_full = lax.all_gather(w_down, ("dp", "blk"), axis=0, tiled=True)
    norm_gain_pair = gain_full.astype(f32)
    norm_offset_pair = shift_full.astype(f32)
    qvb = qvb_full.astype(f32)
    bias_row = jnp.concatenate([qvb[0], jnp.zeros((width,), f32), qvb[1]])
    qkv = (jnp.dot(tokens, wq_full, preferred_element_type=f32) + bias_row).astype(bf16)
    query = qkv[:, :width]
    kv = lax.all_gather(qkv[:, width:], "blk", axis=0, tiled=True)
    attn, lse = attend(query, kv)
    first_hidden = (
        tokens.astype(f32)
        + jnp.dot(attn, wo_full, preferred_element_type=f32)
        + bo_full.astype(f32)
    )
    first_norm_output, first_normalized, first_inverse_deviation = layernorm_forward(
        first_hidden, norm_gain_pair[0], norm_offset_pair[0]
    )
    y1_low = first_norm_output.astype(bf16)
    up = jnp.dot(y1_low, wu_full, preferred_element_type=f32) + bu_full.astype(f32)
    act = jax.nn.gelu(up, approximate=False).astype(bf16)
    second_hidden = (
        first_norm_output + jnp.dot(act, wd_full, preferred_element_type=f32) + bd_full.astype(f32)
    )
    output_float, second_normalized, second_inverse_deviation = layernorm_forward(
        second_hidden, norm_gain_pair[1], norm_offset_pair[1]
    )
    output = output_float.astype(bf16)
    wq_b, wo_b, wu_b, wd_b = wq_full, wo_full, wu_full, wd_full
    gain_pair_block = norm_gain_pair
    incoming_gradient = cotangent.astype(f32)
    second_gain_gradient = jnp.sum(incoming_gradient * second_normalized, axis=0)
    d_shift2 = jnp.sum(incoming_gradient, axis=0)
    second_hidden_gradient = layernorm_backward(
        incoming_gradient, second_normalized, second_inverse_deviation, gain_pair_block[1]
    )
    dh2_low = second_hidden_gradient.astype(bf16)
    d_w_down = contract_rows(act, dh2_low)
    d_down_bias = jnp.sum(second_hidden_gradient, axis=0)
    d_up_f = contract_cols(dh2_low, wd_b) * gelu_grad(up)
    d_up_bias = jnp.sum(d_up_f, axis=0)
    d_up = d_up_f.astype(bf16)
    d_w_up = contract_rows(y1_low, d_up)
    first_output_gradient = second_hidden_gradient + contract_cols(d_up, wu_b)
    first_gain_gradient = jnp.sum(first_output_gradient * first_normalized, axis=0)
    d_shift1 = jnp.sum(first_output_gradient, axis=0)
    first_hidden_gradient = layernorm_backward(
        first_output_gradient, first_normalized, first_inverse_deviation, gain_pair_block[0]
    )
    dh1_low = first_hidden_gradient.astype(bf16)
    d_w_out = contract_rows(attn, dh1_low)
    d_out_bias = jnp.sum(first_hidden_gradient, axis=0)
    d_gains = jnp.stack([first_gain_gradient, second_gain_gradient])
    d_shifts = jnp.stack([d_shift1, d_shift2])
    d_attn = contract_cols(dh1_low, wo_b).astype(bf16)
    delta = jnp.sum((d_attn.astype(f32) * attn.astype(f32)).reshape(rows, heads, HEAD), axis=-1).T
    d_query, d_kv_all = attend_back(
        query, kv, d_attn, lse.transpose(0, 2, 1), delta.reshape(heads // 2, 2, rows)
    )
    d_kv = lax.psum_scatter(d_kv_all, "blk", scatter_dimension=0, tiled=True).astype(f32)
    d_key = d_kv[:, :width]
    d_value = d_kv[:, width:]
    d_qv = jnp.stack([jnp.sum(d_query, axis=0), jnp.sum(d_value, axis=0)])
    d_qkv = jnp.concatenate([d_query, d_key, d_value], axis=1).astype(bf16)
    d_w_qkv = contract_rows(tokens, d_qkv)
    d_tokens = first_hidden_gradient + contract_cols(d_qkv, wq_b)
    grads = [d_qv, d_out_bias[None], d_gains, d_shifts, d_up_bias[None], d_down_bias[None]]
    row = jnp.concatenate([split_owner(v, n) for v in grads], axis=1)
    row = jnp.pad(row[:, None], ((0, 0), (0, SPARE - 1), (0, wide - row.shape[1])))
    packed = jnp.concatenate([d_w_qkv.reshape(n, own_rows, wide), row], axis=1).astype(bf16)

    def to_owner(v):
        return lax.psum_scatter(v, ("dp", "blk"), scatter_dimension=0, tiled=True).astype(f32)

    g_wdown = to_owner(d_w_down.astype(bf16))
    g_wup = to_owner(d_w_up.astype(bf16))
    g_wout = to_owner(d_w_out.astype(bf16))
    packed = to_owner(packed)[0]
    g_wqkv = packed[:own_rows]
    row, at, parts = packed[own_rows], 0, []
    for size, v in zip(sizes, small):
        parts.append(row[at : at + size].reshape(v.shape))
        at += size
    g_qv, g_bout, g_gain, g_shift, g_bup, g_bdown = parts
    return (
        output,
        d_tokens,
        g_wqkv,
        g_qv,
        g_wout,
        g_bout,
        g_gain,
        g_shift,
        g_wup,
        g_bup,
        g_wdown,
        g_bdown,
    )


def solution(mesh):
    return jax.shard_map(
        on_device,
        mesh=mesh,
        in_specs=(
            P(("dp", "blk"), None),
            P(("dp", "blk"), None),
            P(None, ("dp", "blk")),
            P(("dp", "blk"), None),
            P(("dp", "blk")),
            P(None, ("dp", "blk")),
            P(None, ("dp", "blk")),
            P(("dp", "blk"), None),
            P(("dp", "blk")),
            P(("dp", "blk"), None),
            P(("dp", "blk")),
            P(("dp", "blk"), None),
        ),
        out_specs=(
            P(("dp", "blk"), None),
            P(("dp", "blk"), None),
            P(("dp", "blk"), None),
            P(None, ("dp", "blk")),
            P(("dp", "blk"), None),
            P(("dp", "blk")),
            P(None, ("dp", "blk")),
            P(None, ("dp", "blk")),
            P(("dp", "blk"), None),
            P(("dp", "blk")),
            P(("dp", "blk"), None),
            P(("dp", "blk")),
        ),
        check_vma=False,
    )
```

time: 1070 us -> 891 us (0.83)
  blocking collectives: 279 us -> 0 us
  waiting for transfers between devices: 540 us -> 730 us
  matrix products: 166 us -> 39.1 us
  local copies, waits for them, and re-layouts: 35.1 us -> 58.7 us
  Pallas kernels: 0 us -> 19.8 us
    all_gather x6 -> x5, waiting for transfers between devices: 36.8 us -> 267 us  [the longest x1 66.5 us: on_device(): lax.all_gather(jnp.concatenate([w_qkv, row]), ('dp', 'blk'), axis=0)]
    all_gather x3 -> x0, blocking collectives: 200 us -> none  [the longest x1 70.1 us: on_device(): lax.all_gather(qv_bias, ('dp', 'blk'), axis=1, tiled=True)]
    unnamed x13 -> x10, waiting for transfers between devices: 184 us -> 1.85 us
    reduce_scatter x3 -> x5, waiting for transfers between devices: 319 us -> 462 us  [the longest x4 418 us: to_owner(): lax.psum_scatter(v, ('dp', 'blk'), scatter_dimension=0, tiled=True)]
    unnamed x2 -> x0, blocking collectives: 79.4 us -> none
    dot_general x28 -> x4, matrix products: 63.1 us -> 14.7 us  [contract_rows(): lax.dot_general(left, right, (((0,), (0,)), ((), ())), preferred_element_...]
    dot_general x40 -> x4, matrix products: 55.1 us -> 9.27 us  [contract_cols(): lax.dot_general(left, right, (((1,), (1,)), ((), ())), preferred_element_...]
    dot_general x24 -> x0, matrix products: 32 us -> none  [the longest x12 16.1 us: per_head(): part = jnp.dot(weights.astype(bf16), v_h, preferred_element_type=f32)]
  transfers between devices with their start and end apart: 11 -> 10, of which waited for: 6 -> 10; matrix products, arithmetic and copies ran while one was open for 10% -> 9% of each run, Pallas kernels for 0% -> 1%
where the time goes in v1:
time: 891 us; the launch traced here: 888 us
  waiting for transfers between devices  730 us (82%)
  local copies, waits for them, and re-layouts  58.7 us (7%)
  matrix products  39.1 us (4%)
  other arithmetic  25 us (3%)
  Pallas kernels  19.8 us (2%)
  between operations  14.5 us (2%)
    reduce_scatter x4, waiting for transfers between devices, to_owner(): lax.psum_scatter(v, ('dp', 'blk'), scatter_dimension=0, tiled=True)  418 us
    all_gather x1, waiting for transfers between devices, on_device(): lax.all_gather(jnp.concatenate([w_qkv, row]), ('dp', 'blk'), axis=0)  66.5 us
    all_gather x1, waiting for transfers between devices, on_device(): wu_full = lax.all_gather(w_up, ('dp', 'blk'), axis=0, tiled=True)  62.2 us
    all_gather x1, waiting for transfers between devices, on_device(): wd_full = lax.all_gather(w_down, ('dp', 'blk'), axis=0, tiled=True)  56.7 us
    all_gather x1, waiting for transfers between devices, on_device(): wo_full = lax.all_gather(w_out, ('dp', 'blk'), axis=0, tiled=True)  45.1 us
    reduce_scatter x1, waiting for transfers between devices, on_device(): lax.psum_scatter(d_kv_all, 'blk', scatter_dimension=0, tiled=True)  43.3 us
    all_gather x1, waiting for transfers between devices, on_device(): kv = lax.all_gather(qkv[:, width:], 'blk', axis=0, tiled=True)  36.7 us
  transfers between devices with their start and end apart: 10, of which 10 were waited for; matrix products, arithmetic and copies ran while one was open for 9% of the time, Pallas kernels for 1%

profile of v1, /device:TPU:0, one launch (start us, length us, event | category | flops | bytes accessed | tf_op | source)
XLA Modules:
  0.0 888.1 jit_solution(8300312632474955246)
XLA Ops:
  9.4 2.1 concatenate.28
  13.2 66.5 %all-gather.15.cloned.1.call-done = bf16[1024,2304]{1,0:T(8,128)(2,1)} async-done(((bf16[32,2304]{1,0:T(8,128)(2,1)}), bf16[1024,2304]{1,0:T(8,128)(2,1)}) %all-gather.15.cloned.1.call-update) | async-done | bytes 4718608 | tf_op jit(solution)/shard_map/all_gather | solution.py:178
  81.1 2.2 slice.137
  90.3 1.6 fusion.3
  95.5 1.6 slice.142.q_ref
  115.4 36.7 %all-gather.7.cloned.1.call-done.kv_ref = bf16[1024,1536]{1,0:T(8,128)(2,1)} async-done(((bf16[128,1536]{1,0:T(8,128)(2,1)}), bf16[1024,1536]{1,0:T(8,128)(2,1)}) %all-gather.7.cloned.1.call-update) | async-done | bytes 3145744 | tf_op jit(solution)/shard_map/all_gather | solution.py:196
  152.1 9.0 %shard_map.211 = (bf16[128,768]{1,0:T(8,128)(2,1)}, f32[6,128,2]{2,1,0:T(8,128)}) custom-call(bf16[128,768]{1,0:T(8,128)(2,1)} %slice.142.q_ref, bf16[1024,1536]{1,0:T(8,128)(2,1)} %all-gather.7.cloned.1.call-done.kv_ref), custom_call_target="tpu_custom_call" | custom-call | tf_op jit(solution)/shard_map/pallas_call | solution.py:83
  161.1 1.7 copy.55
  162.8 45.1 %all-gather.9.cloned.1.call-done = bf16[768,768]{1,0:T(8,128)(2,1)} async-done(((bf16[24,768]{1,0:T(8,128)(2,1)}), bf16[768,768]{1,0:T(8,128)(2,1)}) %all-gather.9.cloned.1.call-update) | async-done | bytes 1179664 | tf_op jit(solution)/shard_map/all_gather | solution.py:187
  207.9 1.8 fusion.47
  211.1 62.2 %all-gather.11.cloned.1.call-done = bf16[768,3072]{1,0:T(8,128)(2,1)} async-done(((bf16[24,3072]{1,0:T(8,128)(2,1)}), bf16[768,3072]{1,0:T(8,128)(2,1)}) %all-gather.11.cloned.1.call-update) | async-done | bytes 4718608 | tf_op jit(solution)/shard_map/all_gather | solution.py:188
  273.3 8.1 fusion.6
  281.3 56.7 %all-gather.13.cloned.1.call-done = bf16[3072,768]{1,0:T(8,128)(2,1)} async-done(((bf16[96,768]{1,0:T(8,128)(2,1)}), bf16[3072,768]{1,0:T(8,128)(2,1)}) %all-gather.13.cloned.1.call-update) | async-done | bytes 4718608 | tf_op jit(solution)/shard_map/all_gather | solution.py:189
  338.1 3.7 fusion.48
  344.4 2.3 fusion.49
  346.7 2.3 multiply_reduce_fusion
  352.0 1.9 copy.56
  355.5 10.8 %shard_map.212 = (f32[128,768]{1,0:T(8,128)}, bf16[1024,1536]{1,0:T(8,128)(2,1)}) custom-call(bf16[128,768]{1,0:T(8,128)(2,1)} %slice.142.q_ref, bf16[1024,1536]{1,0:T(8,128)(2,1)} %all-gather.7.cloned.1.call-done.kv_ref, bf16[128,768]{1,0:T(8,128)(2,1)} %get-tuple-element.58.do_ref, f32[6,2,128]{2,1,0:T(2,128)} %bitcast.77, f32[6,2,128]{2,1,0:T(2,128)} %reshape.194.delta_ref), custom_call_target="tpu_custom_call" | custom-call | tf_op jit(solution)/shard_map/pallas_call | solution.py:129
  366.4 2.7 convolution_convert_fusion.3
  369.3 4.9 convolution_convert_fusion.1
  374.3 4.9 convolution_convert_fusion
  384.3 1.8 fusion.43
  395.9 43.3 %reduce-scatter.6.cloned.1.call-done = bf16[128,1536]{1,0:T(8,128)(2,1)} async-done(((bf16[1024,1536]{1,0:T(8,128)(2,1)}), bf16[128,1536]{1,0:T(8,128)(2,1)}) %reduce-scatter.6.cloned.1.call-update) | async-done | bytes 393232 | tf_op jit(solution)/shard_map/reduce_scatter | solution.py:247
  445.2 2.3 convolution_convert_fusion.2
  447.5 2.7 fusion.1
  450.2 90.3 %reduce-scatter.10.cloned.1.call-done = bf16[24,768]{1,0:T(8,128)(2,1)} async-done(((bf16[768,768]{1,0:T(8,128)(2,1)}), bf16[24,768]{1,0:T(8,128)(2,1)}) %reduce-scatter.10.cloned.1.call-update) | async-done | bytes 36880 | tf_op jit(solution)/shard_map/reduce_scatter | solution.py:260
  541.9 110.9 %reduce-scatter.12.cloned.1.call-done = bf16[24,3072]{1,0:T(8,128)(2,1)} async-done(((bf16[768,3072]{1,0:T(8,128)(2,1)}), bf16[24,3072]{1,0:T(8,128)(2,1)}) %reduce-scatter.12.cloned.1.call-update) | async-done | bytes 147472 | tf_op jit(solution)/shard_map/reduce_scatter | solution.py:260
  652.8 1.6 convert_element_type.159
  654.4 110.3 %reduce-scatter.14.cloned.1.call-done = bf16[96,768]{1,0:T(8,128)(2,1)} async-done(((bf16[3072,768]{1,0:T(8,128)(2,1)}), bf16[96,768]{1,0:T(8,128)(2,1)}) %reduce-scatter.14.cloned.1.call-update) | async-done | bytes 147472 | tf_op jit(solution)/shard_map/reduce_scatter | solution.py:260
  764.7 1.6 convert_element_type.161
  766.4 3.2 convolution_add_fusion.3
  769.6 106.9 %reduce-scatter.8.cloned.1.call-done = bf16[1,32,2304]{2,1,0:T(8,128)(2,1)} async-done(((bf16[32,32,2304]{2,1,0:T(8,128)(2,1)}), bf16[1,32,2304]{2,1,0:T(8,128)(2,1)}) %reduce-scatter.8.cloned.1.call-update) | async-done | bytes 147472 | tf_op jit(solution)/shard_map/reduce_scatter | solution.py:260
  (156 shorter events, 70.1 us)
Async XLA Ops:
  7.2 72.5 %all-gather.15.cloned.1.call-start = ((), (), s32[]{:S(2)}) async-start(), calls=%async_computation.14 | async-start | bytes 4866048 | tf_op jit(solution)/shard_map/all_gather | solution.py:178
  13.1 139.0 %all-gather.7.cloned.1.call-start = ((), (), s32[]{:S(2)}) async-start(), calls=%async_computation.5 | async-start | bytes 3538944 | tf_op jit(solution)/shard_map/all_gather | solution.py:196
  93.5 114.4 %all-gather.9.cloned.1.call-start = ((), (), s32[]{:S(2)}) async-start(), calls=%async_computation.6 | async-start | bytes 1216512 | tf_op jit(solution)/shard_map/all_gather | solution.py:187
  94.3 179.0 %all-gather.11.cloned.1.call-start = ((), (), s32[]{:S(2)}) async-start(), calls=%async_computation.7 | async-start | bytes 4866048 | tf_op jit(solution)/shard_map/all_gather | solution.py:188
  94.8 243.2 %all-gather.13.cloned.1.call-start = ((), (), s32[]{:S(2)}) async-start(), calls=%async_computation.8 | async-start | bytes 4866048 | tf_op jit(solution)/shard_map/all_gather | solution.py:189
  95.4 343.7 %reduce-scatter.6.cloned.1.call-start = ((), (), s32[]{:S(2)}) async-start(), calls=%async_computation.9 | async-start | bytes 3538944 | tf_op jit(solution)/shard_map/reduce_scatter | solution.py:247
  115.4 92.5 %copy-start.15 = (f32[768]{0:T(1024)S(1)}, f32[768]{0:T(1024)}, u32[]{:S(2)}) copy-start(f32[768]{0:T(1024)} %reshape.202) | copy-start | bytes 9220
  209.7 139.4 %copy-start.11 = (f32[128]{0:T(128)}, f32[128]{0:T(128)S(1)}, u32[]{:S(2)}) copy-start(f32[128]{0:T(128)S(1)} %broadcast_multiply_fusion.5) | copy-start | bytes 1540
  211.1 127.0 %copy-start.13 = (f32[768]{0:T(1024)S(1)}, f32[768]{0:T(1024)}, u32[]{:S(2)}) copy-start(f32[768]{0:T(1024)} %reshape.204) | copy-start | bytes 9220
  338.1 6.2 slice-start.2
  338.1 3.9 copy-start.8
  338.1 3.9 copy-start.10
  338.1 4.7 copy-start.14
  338.1 6.2 slice-start.3
  341.8 2.5 copy-start.22
  342.8 3.9 slice-start
  344.3 2.4 copy-start.4
  344.3 2.4 copy-start.1
  344.3 2.4 slice-start.1
  344.3 2.4 copy-start.16
  346.7 2.4 copy-start.5
  346.7 3.9 copy-start.7
  366.3 3.0 copy-start.12
  366.3 3.0 copy-start.17
  366.3 174.2 %reduce-scatter.10.cloned.1.call-start = ((), (), s32[]{:S(2)}) async-start(), calls=%async_computation.11 | async-start | bytes 1216512 | tf_op jit(solution)/shard_map/reduce_scatter | solution.py:260
  369.1 283.7 %reduce-scatter.12.cloned.1.call-start = ((), (), s32[]{:S(2)}) async-start(), calls=%async_computation.12 | async-start | bytes 4866048 | tf_op jit(solution)/shard_map/reduce_scatter | solution.py:260
  374.3 390.4 %reduce-scatter.14.cloned.1.call-start = ((), (), s32[]{:S(2)}) async-start(), calls=%async_computation.13 | async-start | bytes 4866048 | tf_op jit(solution)/shard_map/reduce_scatter | solution.py:260
  379.2 3.0 copy-start.19
  379.2 7.6 copy-start.21
  379.2 8.3 copy-start.18
  379.2 9.0 %copy-start.20 = (bf16[768]{0:T(1024)(128)(2,1)S(1)}, bf16[768]{0:T(1024)(128)(2,1)}, u32[]{:S(2)}) copy-start(bf16[768]{0:T(1024)(128)(2,1)} %get-tuple-element.20) | copy-start | bytes 4612
  379.3 497.2 %reduce-scatter.8.cloned.1.call-start = ((), (), s32[]{:S(2)}) async-start(), calls=%async_computation.10 | async-start | bytes 4866048 | tf_op jit(solution)/shard_map/reduce_scatter | solution.py:260
  (5 other events, 4.6 us)
Sparse Core Ops, SparseCore 0:
  13.3 66.3 all-gather.14
  93.6 58.3 all-gather.6
  155.1 52.7 all-gather.8
  210.7 62.5 all-gather.10
  276.1 61.9 all-gather.12
  366.4 72.6 reduce-scatter.5
  444.2 96.2 reduce-scatter.9
  546.0 106.7 reduce-scatter.11
  658.3 106.4 reduce-scatter.13
  770.0 106.3 reduce-scatter.7

commit v2 on v1

--- a/solution.py
+++ b/solution.py
@@ -138,7 +138,7 @@
     )(query, kv, d_attn, lse, delta)
 
 
-SPARE = 8
+SPARE = 16
 
 
 def split_owner(full, count):
@@ -170,23 +170,31 @@
     rows, width = tokens.shape
     heads = width // HEAD
     n = lax.axis_size("dp") * lax.axis_size("blk")
-    own_rows, wide = w_qkv.shape
     small = [qv_bias, out_bias, norm_gain, norm_bias, up_bias, down_bias]
     sizes = [v.size for v in small]
-    row = jnp.concatenate([v.reshape(-1) for v in small])
-    row = jnp.pad(row[None], ((0, SPARE - 1), (0, wide - row.size)))
-    packed = lax.all_gather(jnp.concatenate([w_qkv, row]), ("dp", "blk"), axis=0)
-    wq_full = packed[:, :own_rows].reshape(width, wide)
-    row_full = packed[:, own_rows]
+    flat = jnp.concatenate([v.reshape(-1) for v in small])
+    flat = jnp.pad(flat, (0, SPARE * width - flat.size)).reshape(SPARE, width)
+    large = [w_qkv, w_out, w_up, w_down]
+    shard = jnp.concatenate(
+        [v[:, i : i + width] for v in large for i in range(0, v.shape[1], width)] + [flat]
+    )
+    packed = lax.all_gather(shard, ("dp", "blk"), axis=0)
+    wholes, at = [], 0
+    for v in large:
+        high, columns = v.shape
+        blocks = []
+        for _ in range(columns // width):
+            blocks.append(packed[:, at : at + high].reshape(n * high, width))
+            at += high
+        wholes.append(jnp.concatenate(blocks, axis=1))
+    wq_full, wo_full, wu_full, wd_full = wholes
+    row_full = packed[:, at:].reshape(n, -1)
     parts, at = [], 0
     for size, v in zip(sizes, small):
         parts.append(join_owner(row_full[:, at : at + size], 2 if v.ndim == 2 else 1))
         at += size
     qvb_full, bo_full, gain_full, shift_full, bu_full, bd_full = parts
     bo_full, bu_full, bd_full = bo_full[0], bu_full[0], bd_full[0]
-    wo_full = lax.all_gather(w_out, ("dp", "blk"), axis=0, tiled=True)
-    wu_full = lax.all_gather(w_up, ("dp", "blk"), axis=0, tiled=True)
-    wd_full = lax.all_gather(w_down, ("dp", "blk"), axis=0, tiled=True)
     norm_gain_pair = gain_full.astype(f32)
     norm_offset_pair = shift_full.astype(f32)
     qvb = qvb_full.astype(f32)
@@ -253,18 +261,23 @@
     d_tokens = first_hidden_gradient + contract_cols(d_qkv, wq_b)
     grads = [d_qv, d_out_bias[None], d_gains, d_shifts, d_up_bias[None], d_down_bias[None]]
     row = jnp.concatenate([split_owner(v, n) for v in grads], axis=1)
-    row = jnp.pad(row[:, None], ((0, 0), (0, SPARE - 1), (0, wide - row.shape[1])))
-    packed = jnp.concatenate([d_w_qkv.reshape(n, own_rows, wide), row], axis=1).astype(bf16)
-
-    def to_owner(v):
-        return lax.psum_scatter(v, ("dp", "blk"), scatter_dimension=0, tiled=True).astype(f32)
-
-    g_wdown = to_owner(d_w_down.astype(bf16))
-    g_wup = to_owner(d_w_up.astype(bf16))
-    g_wout = to_owner(d_w_out.astype(bf16))
-    packed = to_owner(packed)[0]
-    g_wqkv = packed[:own_rows]
-    row, at, parts = packed[own_rows], 0, []
+    row = jnp.pad(row, ((0, 0), (0, SPARE * width - row.shape[1]))).reshape(n, SPARE, width)
+    blocks = []
+    for d_full, v in zip((d_w_qkv, d_w_out, d_w_up, d_w_down), large):
+        d_low = d_full.astype(bf16).reshape((n,) + v.shape)
+        blocks += [d_low[:, :, i : i + width] for i in range(0, v.shape[1], width)]
+    packed = jnp.concatenate(blocks + [row.astype(bf16)], axis=1)
+    packed = lax.psum_scatter(packed, ("dp", "blk"), scatter_dimension=0, tiled=True)[0]
+    wholes, at = [], 0
+    for v in large:
+        high, columns = v.shape
+        blocks = []
+        for _ in range(columns // width):
+            blocks.append(packed[at : at + high])
+            at += high
+        wholes.append(jnp.concatenate(blocks, axis=1).astype(f32))
+    g_wqkv, g_wout, g_wup, g_wdown = wholes
+    row, at, parts = packed[at:].reshape(-1).astype(f32), 0, []
     for size, v in zip(sizes, small):
         parts.append(row[at : at + size].reshape(v.shape))
         at += size

time: 891 us -> 520 us (0.58)
  waiting for transfers between devices: 730 us -> 381 us
  other arithmetic: 25 us -> 11.9 us
  matrix products: 39.1 us -> 29.4 us
    reduce_scatter x4 -> x1, waiting for transfers between devices: 418 us -> 162 us  [on_device(): lax.psum_scatter(packed, ('dp', 'blk'), scatter_dimension=0, tiled=True)[0]]
    all_gather x4 -> x1, waiting for transfers between devices: 230 us -> 109 us  [on_device(): packed = lax.all_gather(shard, ('dp', 'blk'), axis=0)]
    unnamed x56 -> x102, local copies, waits for them, and re-layouts: 3.85 us -> 25.2 us
    reduce_scatter x1, waiting for transfers between devices: 43.3 us -> 60.6 us  [on_device(): lax.psum_scatter(d_kv_all, 'blk', scatter_dimension=0, tiled=True)]
    all_gather x1, waiting for transfers between devices: 36.7 us -> 49.3 us  [on_device(): kv = lax.all_gather(qkv[:, width:], 'blk', axis=0, tiled=True)]
  transfers between devices with their start and end apart: 10 -> 4, of which waited for: 10 -> 4; matrix products, arithmetic and copies ran while one was open for 9% -> 5% of each run, Pallas kernels for 1% -> 0%
where the time goes in v2:
time: 520 us; the launch traced here: 518 us
  waiting for transfers between devices  381 us (73%)
  local copies, waits for them, and re-layouts  61.1 us (12%)
  matrix products  29.4 us (6%)
  Pallas kernels  19.8 us (4%)
  between operations  14.5 us (3%)
  other arithmetic  11.9 us (2%)
    reduce_scatter x1, waiting for transfers between devices, on_device(): lax.psum_scatter(packed, ('dp', 'blk'), scatter_dimension=0, tiled=True)[0]  162 us
    all_gather x1, waiting for transfers between devices, on_device(): packed = lax.all_gather(shard, ('dp', 'blk'), axis=0)  109 us
    reduce_scatter x1, waiting for transfers between devices, on_device(): lax.psum_scatter(d_kv_all, 'blk', scatter_dimension=0, tiled=True)  60.6 us
    all_gather x1, waiting for transfers between devices, on_device(): kv = lax.all_gather(qkv[:, width:], 'blk', axis=0, tiled=True)  49.3 us
    unnamed x102, local copies, waits for them, and re-layouts  25.2 us
    slice x2, local copies, waits for them, and re-layouts, on_device(): blocks.append(packed[:, at:at + high].reshape(n * high, width))  11.2 us
    pallas_call x1, Pallas kernels, attend_back(): pl.pallas_call(functools.partial(attend_back_kernel, width), out_shape=(j...  10.8 us
  transfers between devices with their start and end apart: 4, of which 4 were waited for; matrix products, arithmetic and copies ran while one was open for 5% of the time, Pallas kernels for 0%

profile of v2, /device:TPU:0, one launch (start us, length us, event | category | flops | bytes accessed | tf_op | source)
XLA Modules:
  0.0 518.0 jit_solution(12715196041650142708)
XLA Ops:
  15.6 2.1 concatenate.39
  19.6 108.7 %all-gather.6.cloned.1.call-done = bf16[9728,768]{1,0:T(8,128)(2,1)} async-done(((bf16[304,768]{1,0:T(8,128)(2,1)}), bf16[9728,768]{1,0:T(8,128)(2,1)}) %all-gather.6.cloned.1.call-update) | async-done | bytes 14942224 | tf_op jit(solution)/shard_map/all_gather | solution.py:181
  128.3 1.2 slice.271
  129.5 6.4 %fusion.46 = (bf16[32,24,768]{2,1,0:T(8,128)(2,1)S(1)}, bf16[32,24,768]{2,1,0:T(8,128)(2,1)}, bf16[32,24,768]{2,1,0:T(8,128)(2,1)}, bf16[32,24,768]{2,1,0:T(8,12...) fusion(bf16[32,304,768]{2,1,0:T(8,128)(2,1)} %bitcast.94), kind=kLoop, calls=%fused_computation.131 | loop fusion | bytes 18874368 | tf_op jit(solution)/shard_map/slice | solution.py:187
  136.2 1.2 copy-done.11
  138.7 1.3 fusion.52
  143.7 2.0 fusion.1
  147.4 1.6 slice.275.q_ref
  149.0 4.8 slice.288
  156.5 49.3 %all-gather.4.cloned.1.call-done.kv_ref = bf16[1024,1536]{1,0:T(8,128)(2,1)} async-done(((bf16[128,1536]{1,0:T(8,128)(2,1)}), bf16[1024,1536]{1,0:T(8,128)(2,1)}) %all-gather.4.cloned.1.call-update) | async-done | bytes 3145744 | tf_op jit(solution)/shard_map/all_gather | solution.py:204
  205.9 9.0 %shard_map.211 = (bf16[128,768]{1,0:T(8,128)(2,1)}, f32[6,128,2]{2,1,0:T(8,128)}) custom-call(bf16[128,768]{1,0:T(8,128)(2,1)} %slice.275.q_ref, bf16[1024,1536]{1,0:T(8,128)(2,1)} %all-gather.4.cloned.1.call-done.kv_ref), custom_call_target="tpu_custom_call" | custom-call | tf_op jit(solution)/shard_map/pallas_call | solution.py:83
  214.9 1.5 fusion.53
  216.7 5.8 %fusion.4 = (bf16[128,3072]{1,0:T(8,128)(2,1)S(1)}, f32[128,3072]{1,0:T(8,128)S(1)}) fusion(f32[3072]{0:T(1024)S(1)} %reshape.261, bf16[768,768]{1,0:T(8,128)(2,1)S(1)} %bitcast.109, bf16[768,768]{1,0:T(8,128)(2,1)S(1)} %bitcast.111, bf16[768,768]{1,0:T(8,128)(2,1)} %bitcast.113, bf16[768,768]{1,0:T(8,128)(2,1)} %bitcast.115, ...), kind=kOutput, calls=%fused_computation.14 | convolution fusion | flops 649297920 | bytes 7490560 | tf_op jit(solution)/shard_map/dot_general | solution.py:215
  224.4 1.5 fusion.43
  225.9 2.4 fusion.55
  228.2 2.3 multiply_reduce_fusion
  231.3 1.4 convert_multiply_fusion.2
  232.7 1.7 copy.73
  234.4 1.1 copy.74
  236.2 10.8 %shard_map.212 = (f32[128,768]{1,0:T(8,128)}, bf16[1024,1536]{1,0:T(8,128)(2,1)}) custom-call(bf16[128,768]{1,0:T(8,128)(2,1)} %slice.275.q_ref, bf16[1024,1536]{1,0:T(8,128)(2,1)} %all-gather.4.cloned.1.call-done.kv_ref, bf16[128,768]{1,0:T(8,128)(2,1)} %get-tuple-element.74.do_ref, f32[6,2,128]{2,1,0:T(2,128)} %bitcast.127, f32[6,2,128]{2,1,0:T(2,128)} %reshape.252.delta_ref), custom_call_target="tpu_custom_call" | custom-call | tf_op jit(solution)/shard_map/pallas_call | solution.py:129
  252.6 3.5 convolution_convert_fusion
  256.2 3.6 convolution_convert_fusion.1
  259.8 60.6 %reduce-scatter.3.cloned.1.call-done = bf16[128,1536]{1,0:T(8,128)(2,1)} async-done(((bf16[1024,1536]{1,0:T(8,128)(2,1)}), bf16[128,1536]{1,0:T(8,128)(2,1)}) %reduce-scatter.3.cloned.1.call-update) | async-done | bytes 393232 | tf_op jit(solution)/shard_map/reduce_scatter | solution.py:255
  320.4 2.2 convolution_convert_fusion.2
  322.9 1.8 slice-done.1
  325.3 5.3 %copy-done = bf16[32,304,768]{2,1,0:T(8,128)(2,1)} copy-done((bf16[32,304,768]{2,1,0:T(8,128)(2,1)}, bf16[32,304,768]{2,1,0:T(8,128)(2,1)S(1)}, u32[]{:S(2)}) %copy-start) | copy-done | bytes 14942232
  331.2 4.8 constant_dynamic-update-slice_fusion.11
  337.0 1.2 copy-done.4
  338.6 3.3 fusion.19
  341.9 162.3 %reduce-scatter.5.cloned.1.call-done = bf16[1,304,768]{2,1,0:T(8,128)(2,1)} async-done(((bf16[32,304,768]{2,1,0:T(8,128)(2,1)}), bf16[1,304,768]{2,1,0:T(8,128)(2,1)}) %reduce-scatter.5.cloned.1.call-update) | async-done | bytes 466960 | tf_op jit(solution)/shard_map/reduce_scatter | solution.py:270
  506.8 1.5 slice_bitcast_fusion.4
  509.8 1.6 fusion.30
  (186 shorter events, 35.6 us)
Async XLA Ops:
  7.2 121.1 %all-gather.6.cloned.1.call-start = ((), (), s32[]{:S(2)}) async-start(), calls=%async_computation.5 | async-start | bytes 15409152 | tf_op jit(solution)/shard_map/all_gather | solution.py:181
  19.5 186.4 %all-gather.4.cloned.1.call-start = ((), (), s32[]{:S(2)}) async-start(), calls=%async_computation.2 | async-start | bytes 3538944 | tf_op jit(solution)/shard_map/all_gather | solution.py:204
  135.9 9.8 %copy-start.3 = (bf16[32,24,768]{2,1,0:T(8,128)(2,1)}, bf16[32,24,768]{2,1,0:T(8,128)(2,1)S(1)}, u32[]{:S(2)}) copy-start(bf16[32,24,768]{2,1,0:T(8,128)(2,1)S(1)} %get-tuple-element.36) | copy-start | bytes 3538948
  135.9 9.8 %copy-start.5 = (bf16[32,24,768]{2,1,0:T(8,128)(2,1)}, bf16[32,24,768]{2,1,0:T(8,128)(2,1)S(1)}, u32[]{:S(2)}) copy-start(bf16[32,24,768]{2,1,0:T(8,128)(2,1)S(1)} %get-tuple-element.37) | copy-start | bytes 3538948
  147.4 173.0 %reduce-scatter.3.cloned.1.call-start = ((), (), s32[]{:S(2)}) async-start(), calls=%async_computation.3 | async-start | bytes 3538944 | tf_op jit(solution)/shard_map/reduce_scatter | solution.py:255
  149.0 6.6 %copy-start.21 = (f32[32,48]{1,0:T(8,128)S(1)}, f32[32,48]{1,0:T(8,128)}, u32[]{:S(2)}) copy-start(f32[32,48]{1,0:T(8,128)} %get-tuple-element.42) | copy-start | bytes 18436
  149.0 6.9 %copy-start.20 = (f32[32,48]{1,0:T(8,128)S(1)}, f32[32,48]{1,0:T(8,128)}, u32[]{:S(2)}) copy-start(f32[32,48]{1,0:T(8,128)} %get-tuple-element.41) | copy-start | bytes 18436
  156.5 58.4 %copy-start.13 = (bf16[128,768]{1,0:T(8,128)(2,1)S(1)}, bf16[128,768]{1,0:T(8,128)(2,1)}, u32[]{:S(2)}) copy-start(bf16[128,768]{1,0:T(8,128)(2,1)} %param.12) | copy-start | bytes 589828
  214.9 7.6 %slice-start.2 = ((s8[4718592]{0:T(1024)(128)(4,1)}), s8[4194304]{0:T(1024)(128)(4,1)S(1)}, s32[]{:S(2)}) async-start(s8[4718592]{0:T(1024)(128)(4,1)} %bitcast.89), calls=%async_computation.8 | async-start | bytes 8388608
  216.4 14.1 %copy-start.27 = (f32[128]{0:T(128)}, f32[128]{0:T(128)S(1)}, u32[]{:S(2)}) copy-start(f32[128]{0:T(128)S(1)} %broadcast_multiply_fusion.5) | copy-start | bytes 1540
  216.6 13.9 %copy-start.29 = (f32[128]{0:T(128)}, f32[128]{0:T(128)S(1)}, u32[]{:S(2)}) copy-start(f32[128]{0:T(128)S(1)} %add_rsqrt_fusion.1) | copy-start | bytes 1540
  216.7 5.8 %slice-start.3 = ((s8[4718592]{0:T(1024)(128)(4,1)}), s8[524288]{0:T(1024)(128)(4,1)S(1)}, s32[]{:S(2)}) async-start(s8[4718592]{0:T(1024)(128)(4,1)} %bitcast.89), calls=%async_computation.9 | async-start | bytes 1048576
  225.9 2.4 copy-start.9
  225.9 2.4 copy-start.10
  228.2 2.3 copy-start.15
  228.2 3.1 copy-start.1
  247.0 2.8 copy-start.35
  247.0 3.7 copy-start.34
  247.0 4.4 copy-start.31
  247.1 257.1 %reduce-scatter.5.cloned.1.call-start = ((), (), s32[]{:S(2)}) async-start(), calls=%async_computation.4 | async-start | bytes 15409152 | tf_op jit(solution)/shard_map/reduce_scatter | solution.py:270
  252.6 3.6 copy-start.16
  252.6 3.6 copy-start.28
  252.6 3.6 copy-start.30
  256.2 64.2 %copy-start.14 = (bf16[128,768]{1,0:T(8,128)(2,1)S(1)}, bf16[128,768]{1,0:T(8,128)(2,1)}, u32[]{:S(2)}) copy-start(bf16[128,768]{1,0:T(8,128)(2,1)} %param.12) | copy-start | bytes 589828
  320.4 2.5 slice-start
  325.1 5.4 %copy-start.12 = (bf16[128,1536]{1,0:T(8,128)(2,1)S(1)}, bf16[128,1536]{1,0:T(8,128)(2,1)}, u32[]{:S(2)}) copy-start(bf16[128,1536]{1,0:T(8,128)(2,1)} %reduce-scatter.3.cloned.1.call-done) | copy-start | bytes 1179652
  325.1 5.6 %copy-start.26 = (bf16[1,32,24]{2,1,0:T(8,128)(2,1)S(1)}, bf16[1,32,24]{2,1,0:T(8,128)(2,1)}, u32[]{:S(2)}) copy-start(bf16[1,32,24]{2,1,0:T(8,128)(2,1)} %stack.27) | copy-start | bytes 4612
  325.1 5.8 %copy-start.22 = (bf16[32,96]{1,0:T(8,128)(2,1)S(1)}, bf16[32,96]{1,0:T(8,128)(2,1)}, u32[]{:S(2)}) copy-start(bf16[32,96]{1,0:T(8,128)(2,1)} %reshape_transpose_reshape_broadcast_in_dim.13) | copy-start | bytes 18436
  325.1 5.8 %copy-start.23 = (bf16[32,24]{1,0:T(8,128)(2,1)S(1)}, bf16[32,24]{1,0:T(8,128)(2,1)}, u32[]{:S(2)}) copy-start(bf16[32,24]{1,0:T(8,128)(2,1)} %reshape_transpose_reshape_broadcast_in_dim.14) | copy-start | bytes 4612
  325.1 5.8 %copy-start.24 = (bf16[32,48]{1,0:T(8,128)(2,1)S(1)}, bf16[32,48]{1,0:T(8,128)(2,1)}, u32[]{:S(2)}) copy-start(bf16[32,48]{1,0:T(8,128)(2,1)} %copy.79) | copy-start | bytes 9220
  325.2 5.8 %copy-start.25 = (bf16[32,48]{1,0:T(8,128)(2,1)S(1)}, bf16[32,48]{1,0:T(8,128)(2,1)}, u32[]{:S(2)}) copy-start(bf16[32,48]{1,0:T(8,128)(2,1)} %copy.80) | copy-start | bytes 9220
  325.3 5.3 %copy-start = (bf16[32,304,768]{2,1,0:T(8,128)(2,1)}, bf16[32,304,768]{2,1,0:T(8,128)(2,1)S(1)}, u32[]{:S(2)}) copy-start(bf16[32,304,768]{2,1,0:T(8,128)(2,1)S(1)} %slice_dynamic-update-slice_fusion) | copy-start | bytes 44826628
  (13 other events, 19.0 us)
Sparse Core Ops, SparseCore 0:
  19.6 108.6 all-gather.5
  147.5 58.3 all-gather.3
  247.2 73.1 reduce-scatter.2
  337.1 166.9 reduce-scatter.4
